TPU v7x, 128 devices: a whole 4x4x4 slice. The times are simulated.
128 devices in a mesh: seq: 32 (over y, z, core), head: 4 (over x).
Axes of the slice: x: 4, y: 4, z: 4, core: 2. Of those that a mesh axis runs over, the one named last changes fastest.
Arguments:
- hidden_in: bfloat16 [8192, 2048], P('seq'), may hold values from -6 to 6
- attn_gain: float32 [2048], replicated, may hold values from 0.1 to 1.9
- w_qkv: bfloat16 [2048, 3, 2048], P(None, None, 'head'), may hold values from -0.125 to 0.125
- out_gain: float32 [2048], P('head'), may hold values from 0.1 to 1.9
- w_out: bfloat16 [2048, 2048], P('head'), may hold values from -0.125 to 0.125
- moe_gain: float32 [2048], replicated, may hold values from 0.1 to 1.9
- routes: int32 [8192, 8], P(('seq', 'head')), may hold values from 0 to 63, all different within a row; in each aligned block of 64 rows (0 to 63, 64 to 127, ...) at most 9 rows name the same one
- gate_weights: float32 [8192, 8], P(('seq', 'head')), may hold values from 0.1 to 0.6
- w_gate_up: bfloat16 [64, 2, 2048, 1024], P('seq', None, None, 'head'), may hold values from -0.125 to 0.125
- w_down: bfloat16 [64, 1024, 2048], P('seq', 'head'), may hold values from -0.1875 to 0.1875
Outputs:
- layer_out: bfloat16 [8192, 2048], P(('seq', 'head'))
Inputs may be any that keep to these rules, and one draw needn't show every extreme that they name: `routes`: each row names 8 different experts; within each aligned block of 64 rows (the rows of one device) no expert is named more than 9 times, a bound that some block reaches.
All inputs are finite; a program needn't handle non-finite values.
Results may differ from a plain program's by a relative error of at most 0.015.
Values may be sent and summed in bfloat16 or wider, within the bound.
No kernel may reach another device: no remote copies, remote signals or barrier semaphores. Data moves between devices by JAX's collectives and lax.ppermute only.
A program may use at most 128 MiB of HBM per device.

v0:
```python
import jax
import jax.numpy as jnp
from jax import lax
from jax.experimental import pallas as pl
from jax.experimental.pallas import tpu as pltpu
from jax.sharding import PartitionSpec as P

D = 2048
DH = 128
HEADS = 4
WIDE = HEADS * DH
TOP = 8
CAP = 9
ROWS = 64
TOK = 256
MAIN = 512
SLOTS = 576
PACKED = D + 256
EPSILON = 1e-06
BF = jnp.bfloat16
F32 = jnp.float32


VMEM = pl.BlockSpec(memory_space=pltpu.VMEM)
SMEM = pl.BlockSpec(memory_space=pltpu.SMEM)
ANY = pl.BlockSpec(memory_space=pl.ANY)


def out(shape, dtype):
    return jax.ShapeDtypeStruct(shape, dtype)


def call(kernel, ins, outs, scratch=()):
    return pl.pallas_call(
        kernel,
        in_specs=ins,
        out_specs=[VMEM] * len(outs),
        out_shape=outs,
        scratch_shapes=list(scratch),
        compiler_params=pltpu.CompilerParams(vmem_limit_bytes=56 << 20),
    )


def rms_norm(values, gain):
    mean_square = jnp.mean(values * values, axis=-1, keepdims=True)
    return values * lax.rsqrt(mean_square + EPSILON) * gain


def dot(first, second):
    return jnp.dot(first, second, preferred_element_type=F32)


def dot_rows(first, second):
    return lax.dot_general(first, second, (((0,), (0,)), ((), ())), preferred_element_type=F32)


def dot_cols(first, second):
    return lax.dot_general(first, second, (((1,), (1,)), ((), ())), preferred_element_type=F32)


def of_head(h):
    return slice(h * DH, (h + 1) * DH)


def front_kernel(x_ref, gain_ref, wk_ref, wv_ref, normed_ref, k_ref, v_ref, state_ref, send_ref, wk, wv, sems):
    copy_k = pltpu.make_async_copy(wk_ref, wk, sems.at[0])
    copy_v = pltpu.make_async_copy(wv_ref, wv, sems.at[1])
    copy_k.start()
    copy_v.start()
    normed = rms_norm(x_ref[...].astype(F32), gain_ref[...]).astype(BF)
    normed_ref[...] = normed
    copy_k.wait()
    key = dot(normed, wk[...]).astype(BF)
    k_ref[...] = key
    copy_v.wait()
    value = dot(normed, wv[...]).astype(BF)
    v_ref[...] = value
    for h in range(HEADS):
        state = dot_rows(key[:, of_head(h)], value[:, of_head(h)])
        state_ref[h] = state
        send_ref[h] = state.astype(BF)


def local_kernel(normed_ref, wq_ref, k_ref, v_ref, q_ref, local_ref):
    query = dot(normed_ref[...], wq_ref[...]).astype(BF)
    q_ref[...] = query
    row = lax.broadcasted_iota(jnp.int32, (TOK, TOK), 0)
    causal = lax.broadcasted_iota(jnp.int32, (TOK, TOK), 1) <= row
    for h in range(HEADS):
        scores = dot_cols(query[:, of_head(h)], k_ref[:, of_head(h)])
        scores = jnp.where(causal, scores, 0.0).astype(BF)
        local_ref[:, of_head(h)] = dot(scores, v_ref[:, of_head(h)])


def attend_kernel(
    place_ref, prefix_ref, g1, g2, g3, q_ref, local_ref, gain_ref, w_ref,
    own_ref, s1, s2, s3, mixed_ref, turned_ref,
):
    y = place_ref[0]
    head = place_ref[1]
    for h in range(HEADS):
        earlier = prefix_ref[h]
        for k, got in ((1, g1), (2, g2), (3, g3)):
            earlier = earlier + jnp.where(y >= k, got[h].astype(F32), 0.0)
        high = earlier.astype(BF)
        low = (earlier - high.astype(F32)).astype(BF)
        query = q_ref[:, of_head(h)]
        attended = local_ref[:, of_head(h)] + (dot(query, high) + dot(query, low))
        mixed_ref[:, of_head(h)] = rms_norm(attended, gain_ref[:, of_head(h)]).astype(BF)
    for k in range(4):
        start = pl.multiple_of(((head - k) % 4) * ROWS, ROWS)
        turned_ref[k * ROWS:(k + 1) * ROWS, :] = mixed_ref[pl.ds(start, ROWS), :]
    for n in range(4):
        cols = slice(n * 512, (n + 1) * 512)
        rows = dot(turned_ref[...], w_ref[:, cols])
        own_ref[:, cols] = rows[:ROWS]
        s3[:, cols] = rows[ROWS:2 * ROWS].astype(BF)
        s2[:, cols] = rows[2 * ROWS:3 * ROWS].astype(BF)
        s1[:, cols] = rows[3 * ROWS:].astype(BF)


def dispatch_kernel(place_ref, t0, t1, t2, t3, out_ref, tokens):
    for k, ref in enumerate((t0, t1, t2, t3)):
        tokens[k * ROWS:(k + 1) * ROWS, :] = ref[...]
    tail = []
    for n in range(4):
        cols = slice(n * 512, (n + 1) * 512)
        rows = dot(place_ref[...], tokens[:, cols])
        out_ref[:, cols] = rows[:MAIN].astype(BF)
        tail.append(rows[MAIN:])
    tail = jnp.concatenate(tail, axis=1)
    for t in range(2):
        piece = tail[t * 32:(t + 1) * 32].reshape(MAIN, 128).astype(BF)
        out_ref[:, D + t * 128:D + (t + 1) * 128] = piece


def expert_kernel(x_ref, gu0, gu1, gu2, gu3, dn0, dn1, dn2, dn3, out_ref, rows, ends, gate_up, down, act, tail, sems):
    copies = [
        pltpu.make_async_copy(x_ref.at[:, :D], rows.at[:MAIN], sems.at[8]),
        pltpu.make_async_copy(x_ref.at[:, D:], ends, sems.at[9]),
    ]
    for q, (gu, dn) in enumerate(((gu0, dn0), (gu1, dn1), (gu2, dn2), (gu3, dn3))):
        copies.append(pltpu.make_async_copy(gu, gate_up.at[q], sems.at[q]))
        copies.append(pltpu.make_async_copy(dn, down.at[q * 256:(q + 1) * 256], sems.at[4 + q]))
    for copy in copies:
        copy.start()
    copies[1].wait()
    for t in range(2):
        piece = ends[:, t * 128:(t + 1) * 128].astype(F32).reshape(32, D)
        rows[MAIN + t * 32:MAIN + (t + 1) * 32, :] = piece.astype(BF)
    copies[0].wait()
    for q in range(4):
        copies[2 + 2 * q].wait()
        gate = dot(rows[...], gate_up[q, 0])
        up = dot(rows[...], gate_up[q, 1])
        act[:, q * 256:(q + 1) * 256] = (jax.nn.silu(gate) * up).astype(BF)
    for q in range(4):
        copies[3 + 2 * q].wait()
    for n in range(4):
        cols = slice(n * 512, (n + 1) * 512)
        result = dot(act[...], down[:, cols])
        out_ref[:, cols] = result[:MAIN].astype(BF)
        tail[:, cols] = result[MAIN:]
    for t in range(2):
        piece = tail[t * 32:(t + 1) * 32, :].reshape(MAIN, 128).astype(BF)
        out_ref[:, D + t * 128:D + (t + 1) * 128] = piece


def combine_kernel(weight_ref, y_ref, own_ref, s1, s2, s3, tail):
    for t in range(2):
        piece = y_ref[:, D + t * 128:D + (t + 1) * 128].astype(F32).reshape(32, D)
        tail[t * 32:(t + 1) * 32, :] = piece.astype(BF)
    for n in range(4):
        cols = slice(n * 512, (n + 1) * 512)
        rows = dot(weight_ref[:, :MAIN], y_ref[:, cols]) + dot(weight_ref[:, MAIN:], tail[:, cols])
        rows = rows[:TOK] + rows[TOK:]
        own_ref[:, cols] = rows[:ROWS]
        s3[:, cols] = rows[ROWS:2 * ROWS].astype(BF)
        s2[:, cols] = rows[2 * ROWS:3 * ROWS].astype(BF)
        s1[:, cols] = rows[3 * ROWS:].astype(BF)


BLOCKS_OUT = [out((ROWS, D), F32)] + [out((ROWS, D), BF)] * 3


def seq_perm(dy, dz, dc):
    return [
        ((y * 4 + z) * 2 + c, (((y + dy) % 4) * 4 + (z + dz) % 4) * 2 + (c ^ dc))
        for y in range(4)
        for z in range(4)
        for c in range(2)
    ]


def head_perm(shift):
    return [(h, (h + shift) % 4) for h in range(4)]


def device_perm(target):
    pairs = []
    for chip in range(16):
        for c in range(2):
            for h in range(4):
                to = target(c, h)
                pairs.append(((chip * 2 + c) * 4 + h, (chip * 2 + to[0]) * 4 + to[1]))
    return pairs


def near_target(c, h):
    chip = 2 * c + 1 - (h & 1)
    return (c, chip) if (chip - 1) % 4 == h else (1 - c, chip)


def far_target(c, h):
    return (c, h) if h // 2 == c else (1 - c, (h + 2) % 4)


def permute_all(arrays, axes, perm):
    return [lax.ppermute(a, axes, perm) for a in arrays]


def gather_weights(w_gate_up, w_down, head):
    odd = head & 1

    def pick(index):
        return [
            lax.dynamic_index_in_dim(w_gate_up, index, 0, False),
            lax.dynamic_index_in_dim(w_down, index, 0, False),
        ]

    both = ("seq", "head")
    swap = seq_perm(0, 0, 1)
    near = permute_all(pick(1 - odd), both, device_perm(near_target))
    far = permute_all(pick(odd), both, device_perm(far_target))
    near_other = permute_all(near, "seq", swap)
    far_other = permute_all(far, "seq", swap)
    return [near, near_other, far, far_other]


def exchange(array, step):
    dy, dz = step
    return [lax.ppermute(array, "seq", seq_perm(dy * k, dz * k, 0)) for k in range(1, 4)]


def gather_head(array):
    return [array] + [lax.ppermute(array, "head", head_perm(k)) for k in range(1, 4)]


def scatter_head(blocks):
    total = blocks[0]
    for k in range(1, 4):
        total = total + lax.ppermute(blocks[k], "head", head_perm(k)).astype(F32)
    return total


def on_device(
    hidden_in, attn_gain, w_qkv, out_gain, w_out, moe_gain, routes, gate_weights, w_gate_up, w_down
):
    seq = lax.axis_index("seq")
    head = lax.axis_index("head")
    core = seq % 2
    z = (seq // 2) % 4
    y = seq // 8

    pieces = gather_weights(w_gate_up, w_down, head)
    tables = gather_head(jnp.concatenate([routes.astype(F32), gate_weights], axis=1))
    tables = jnp.concatenate(tables, axis=0)

    normed, key, value, own_state, send_state = call(
        front_kernel,
        [VMEM, VMEM, ANY, ANY],
        [
            out((TOK, D), BF),
            out((TOK, WIDE), BF),
            out((TOK, WIDE), BF),
            out((HEADS, DH, DH), F32),
            out((HEADS, DH, DH), BF),
        ],
        [pltpu.VMEM((D, WIDE), BF), pltpu.VMEM((D, WIDE), BF), pltpu.SemaphoreType.DMA((2,))],
    )(hidden_in, attn_gain[None, :], w_qkv[:, 1], w_qkv[:, 2])
    sibling = lax.ppermute(send_state, "seq", seq_perm(0, 0, 1)).astype(F32)
    prefix = jnp.where(core == 1, sibling, 0.0)
    total = own_state + sibling
    rows_z = exchange(total.astype(BF), (0, 1))
    for k, got in enumerate(rows_z):
        prefix = prefix + jnp.where(z > k, got.astype(F32), 0.0)
        total = total + got.astype(F32)
    rows_y = exchange(total.astype(BF), (1, 0))

    query, local = call(
        local_kernel, [VMEM] * 4, [out((TOK, WIDE), BF), out((TOK, WIDE), F32)]
    )(normed, w_qkv[:, 0], key, value)
    place = jnp.stack([y, head]).astype(jnp.int32)
    blocks = call(
        attend_kernel,
        [SMEM] + [VMEM] * 8,
        BLOCKS_OUT,
        [pltpu.VMEM((TOK, WIDE), BF), pltpu.VMEM((TOK, WIDE), BF)],
    )(place, prefix, *rows_y, query, local, out_gain[None, :], w_out)
    attn_rows = scatter_head(blocks)
    resid = lax.dynamic_slice_in_dim(hidden_in, head * ROWS, ROWS, 0).astype(F32) + attn_rows
    normed2 = rms_norm(resid, moe_gain).astype(BF)
    tokens = gather_head(normed2)

    named = tables[:, :TOP].astype(jnp.int32)
    wanted = jnp.arange(16, dtype=jnp.int32) * 4 + head
    hit = named[:, :, None] == wanted[None, None, :]
    chosen = jnp.sum(hit.astype(F32), axis=1)
    gates = jnp.sum(jnp.where(hit, tables[:, TOP:, None], 0.0), axis=1)
    index = jnp.arange(TOK, dtype=jnp.int32)
    group = index // ROWS
    block = (head - group) % 4
    before = (group[:, None] == group[None, :]) & (index[None, :] < index[:, None])
    rank = dot(before.astype(BF), chosen.astype(BF)).astype(jnp.int32)
    slot = jnp.where(chosen > 0, (block // 2 * 18 + block % 2 * CAP)[:, None] + rank, -1).T
    gates = gates.T
    first = (jnp.arange(2, dtype=jnp.int32) * 18)[:, None] + jnp.arange(16, dtype=jnp.int32)
    last = jnp.arange(2, dtype=jnp.int32)[:, None] + jnp.array([16, 34], jnp.int32)
    main = slot[:, None, None, :] == first[None, :, :, None]
    ends = slot[None, :, None, :] == last[:, None, :, None]
    place_rows = jnp.concatenate([main.reshape(MAIN, TOK), ends.reshape(64, TOK)], axis=0)
    weight = jnp.concatenate(
        [
            jnp.where(main, gates[:, None, None, :], 0.0).reshape(MAIN, TOK),
            jnp.where(ends, gates[None, :, None, :], 0.0).reshape(64, TOK),
        ],
        axis=0,
    ).T
    high = weight.astype(BF)
    low = (weight - high.astype(F32)).astype(BF)
    weight = jnp.concatenate([high, low], axis=0)

    sent = call(
        dispatch_kernel, [VMEM] * 5, [out((MAIN, PACKED), BF)], [pltpu.VMEM((TOK, D), BF)]
    )(place_rows.astype(BF), *tokens)[0]
    received = lax.all_to_all(sent.reshape(32, 16, PACKED), "seq", 0, 0, tiled=True)
    results = call(
        expert_kernel,
        [ANY] * 9,
        [out((MAIN, PACKED), BF)],
        [
            pltpu.VMEM((SLOTS, D), BF),
            pltpu.VMEM((MAIN, 256), BF),
            pltpu.VMEM((4, 2, D, 256), BF),
            pltpu.VMEM((1024, D), BF),
            pltpu.VMEM((SLOTS, 1024), BF),
            pltpu.VMEM((64, D), F32),
            pltpu.SemaphoreType.DMA((10,)),
        ],
    )(received.reshape(MAIN, PACKED), *[p[0] for p in pieces], *[p[1] for p in pieces])[0]
    back = lax.all_to_all(results.reshape(32, 16, PACKED), "seq", 0, 0, tiled=True)
    blocks = call(
        combine_kernel, [VMEM] * 2, BLOCKS_OUT, [pltpu.VMEM((64, D), BF)]
    )(weight, back.reshape(MAIN, PACKED))
    moe_sum = scatter_head(blocks)
    return (resid + moe_sum).astype(BF)


def solution(mesh):
    placed = (
        P("seq", None),
        P(),
        P(None, None, "head"),
        P("head"),
        P("head", None),
        P(),
        P(("seq", "head"), None),
        P(("seq", "head"), None),
        P("seq", None, None, "head"),
        P("seq", "head", None),
    )

    return jax.shard_map(
        on_device, mesh=mesh, in_specs=placed, out_specs=P(("seq", "head"), None), check_vma=False
    )
```

profile of v0, /device:TPU:1, one launch (start us, length us, event | category | flops | bytes accessed | tf_op | source)
XLA Modules:
  0.0 223.4 jit_solution(6043615971749451453)
XLA Ops:
  1.4 3.3 %collective-permute-start.12 = (f32[64,16]{0,1:T(8,128)S(1)}, f32[64,16]{0,1:T(8,128)S(1)}, u32[]{:S(2)}, u32[]{:S(2)}) collective-permute-start(f32[64,16]{0,1:T(8,128)S(1)} %pad_maximum_fusion.2), channel_id=1, source_target_pairs={{0,3},{1,0},{2,1},{3,2},{4,7},{5,4},{6,5},{7,6},{8,11},{9,8},{10,9... | collective-permute-start | bytes 12296 | tf_op jit(solution)/shard_map/ppermute | solution.py:246
  5.8 5.6 %slice_bitcast_fusion = (bf16[2048,512]{1,0:T(8,128)(2,1)}, bf16[2048,512]{1,0:T(8,128)(2,1)}, bf16[2048,512]{1,0:T(8,128)(2,1)}) fusion(bf16[2048,3,512]{2,0,1:T(8,128)(2,1)} %param.13), kind=kLoop, calls=%fused_computation.2 | loop fusion | bytes 12582912 | tf_op jit(solution)/shard_map/squeeze | solution.py:292
  11.4 5.2 %shard_map.109 = (bf16[256,2048]{1,0:T(8,128)(2,1)}, bf16[256,512]{1,0:T(8,128)(2,1)}, bf16[256,512]{1,0:T(8,128)(2,1)}, f32[4,128,128]{2,1,0:T(8,128)}, bf16[4,128,128]{2,1,0:T(8,128)(2,1)}) custom-call(bf16[256,2048]{1,0:T(8,128)(2,1)} %x_ref.1, f32[1,2048]{1,0:T(1,128)} %bitcast.43, bf16[2048,512]{1,0:T(8,128)(2,1)} %get-tuple-element.44.wk_ref, ...), custom_call_target="tpu_custom_call" | custom-call | tf_op jit(solution)/shard_map/pallas_call | solution.py:269
  18.2 4.6 %dynamic-slice_bitcast_fusion = (bf16[2,2048,256]{2,1,0:T(8,128)(2,1)}, bf16[2,2048,256]{2,1,0:T(8,128)(2,1)}) fusion(bf16[2,2,2048,256]{3,2,1,0:T(8,128)(2,1)} %param.19, s32[]{:T(128)S(6)} %select_n.141, s32[]{:T(128)S(6)} %select_n.140), kind=kLoop, calls=%fused_computation | loop fusion | bytes 8388616 | tf_op jit(solution)/shard_map/jit(dynamic_index_in_dim)/squeeze | solution.py:227
  25.8 3.9 %shard_map.110 = (bf16[256,512]{1,0:T(8,128)(2,1)}, f32[256,512]{1,0:T(8,128)}) custom-call(bf16[256,2048]{1,0:T(8,128)(2,1)} %get-tuple-element.22.normed_ref, bf16[2048,512]{1,0:T(8,128)(2,1)} %get-tuple-element.43.wq_ref, bf16[256,512]{1,0:T(8,128)(2,1)} %get-tuple-element.23.k_ref, bf16[256,512]{1,0:T(8,128)(2,1)} %get-tuple-element.24.v_ref), custom_call_target="tpu_custom_call" | custom-call | tf_op jit(solution)/shard_map/pallas_call | solution.py:290
  29.7 3.5 %collective-permute-start.18 = (bf16[2,2048,256]{2,1,0:T(8,128)(2,1)}, bf16[2,2048,256]{2,1,0:T(8,128)(2,1)}, u32[]{:S(2)}, u32[]{:S(2)}) collective-permute-start(bf16[2,2048,256]{2,1,0:T(8,128)(2,1)} %get-tuple-element.46), channel_id=1, source_target_pairs={{0,0},{1,1},{2,4},{3,5},{4,2},{5,3},{6,6},{7,7},{8,8},{9,9},{10,12... | collective-permute-start | bytes 6291464 | tf_op jit(solution)/shard_map/ppermute | solution.py:219
  33.4 3.8 %collective-permute-start.3 = (bf16[4,128,128]{2,1,0:T(8,128)(2,1)S(1)}, bf16[4,128,128]{2,1,0:T(8,128)(2,1)S(1)}, u32[]{:S(2)}, u32[]{:S(2)}) collective-permute-start(bf16[4,128,128]{2,1,0:T(8,128)(2,1)S(1)} %fusion.10), channel_id=1, source_target_pairs={{0,24},{4,28},{8,0},{12,4},{16,8},{20,12},{24,16},{28,20},{32,56},... | collective-permute-start | bytes 393224 | tf_op jit(solution)/shard_map/ppermute | solution.py:242
  53.6 4.3 %shard_map.111 = (f32[64,2048]{1,0:T(8,128)}, bf16[64,2048]{1,0:T(8,128)(2,1)}, bf16[64,2048]{1,0:T(8,128)(2,1)}, bf16[64,2048]{1,0:T(8,128)(2,1)}) custom-call(s32[2]{0:T(128)} %pad_add_fusion.place_ref, f32[4,128,128]{2,1,0:T(8,128)} %get-tuple-element.51.prefix_ref, bf16[4,128,128]{2,1,0:T(8,128)(2,1)} %copy-done.10, bf16[4,128,128]{2,1,0:T(8,128)(2,1)} %copy-done.11, ...), custom_call_target="tpu_custom_call" | custom-call | tf_op jit(solution)/shard_map/pallas_call | solution.py:294
  57.9 13.8 %collective-permute-start.9 = (bf16[64,2048]{1,0:T(8,128)(2,1)}, bf16[64,2048]{1,0:T(8,128)(2,1)S(1)}, u32[]{:S(2)}, u32[]{:S(2)}) collective-permute-start(bf16[64,2048]{1,0:T(8,128)(2,1)} %get-tuple-element.30), channel_id=1, source_target_pairs={{0,3},{1,0},{2,1},{3,2},{4,7},{5,4},{6,5},{7,6},{8,11},{9,8},{10,9... | collective-permute-start | bytes 786440 | tf_op jit(solution)/shard_map/ppermute | solution.py:252
  73.7 5.6 %collective-permute-done.9 = bf16[64,2048]{1,0:T(8,128)(2,1)S(1)} collective-permute-done((bf16[64,2048]{1,0:T(8,128)(2,1)}, bf16[64,2048]{1,0:T(8,128)(2,1)S(1)}, u32[]{:S(2)}, u32[]{:S(2)}) %collective-permute-start.9) | collective-permute-done | bytes 262176 | tf_op jit(solution)/shard_map/ppermute | solution.py:252
  79.3 7.3 %collective-permute-done.7 = bf16[64,2048]{1,0:T(8,128)(2,1)S(1)} collective-permute-done((bf16[64,2048]{1,0:T(8,128)(2,1)}, bf16[64,2048]{1,0:T(8,128)(2,1)S(1)}, u32[]{:S(2)}, u32[]{:S(2)}) %collective-permute-start.7) | collective-permute-done | bytes 262176 | tf_op jit(solution)/shard_map/ppermute | solution.py:252
  92.6 4.8 %collective-permute-done.13.t1 = bf16[64,2048]{1,0:T(8,128)(2,1)S(1)} collective-permute-done((bf16[64,2048]{1,0:T(8,128)(2,1)S(1)}, bf16[64,2048]{1,0:T(8,128)(2,1)S(1)}, u32[]{:S(2)}, u32[]{:S(2)}) %collective-permute-start.13) | collective-permute-done | bytes 262176 | tf_op jit(solution)/shard_map/ppermute | solution.py:246
  97.4 3.0 %collective-permute-done.14.t2 = bf16[64,2048]{1,0:T(8,128)(2,1)S(1)} collective-permute-done((bf16[64,2048]{1,0:T(8,128)(2,1)S(1)}, bf16[64,2048]{1,0:T(8,128)(2,1)S(1)}, u32[]{:S(2)}, u32[]{:S(2)}) %collective-permute-start.14) | collective-permute-done | bytes 262176 | tf_op jit(solution)/shard_map/ppermute | solution.py:246
  103.5 3.5 %shard_map.112 = bf16[512,2304]{1,0:T(8,128)(2,1)} custom-call(bf16[576,256]{1,0:T(8,128)(2,1)} %copy.33.place_ref, bf16[64,2048]{1,0:T(8,128)(2,1)} %copy-done.2, bf16[64,2048]{1,0:T(8,128)(2,1)} %copy-done.7, bf16[64,2048]{1,0:T(8,128)(2,1)} %copy-done.8, bf16[64,2048]{1,0:T(8,128)(2,1)} %copy-done.9), custom_call_target="tpu_custom_call" | custom-call | tf_op jit(solution)/shard_map/pallas_call | solution.py:333
  107.0 6.5 %all-to-all-start = ((bf16[32,16,2304]{2,1,0:T(8,128)(2,1)}), bf16[32,16,2304]{2,1,0:T(8,128)(2,1)S(1)}, u32[]{:S(2)}, u32[]{:S(2)}) async-start(bf16[32,16,2304]{2,1,0:T(8,128)(2,1)} %bitcast.35), calls=%async_computation | async-start | bytes 4718592 | tf_op jit(solution)/shard_map/all_to_all | solution.py:336
  117.6 2.9 %collective-permute-start.22 = (bf16[256,2048]{1,0:T(8,128)(2,1)S(1)}, bf16[256,2048]{1,0:T(8,128)(2,1)S(1)}, u32[]{:S(2)}, u32[]{:S(2)}) collective-permute-start(bf16[256,2048]{1,0:T(8,128)(2,1)S(1)} %get-tuple-element.48), channel_id=1, source_target_pairs={{0,0},{1,1},{2,4},{3,5},{4,2},{5,3},{6,6},{7,7},{8,8},{9,9},{10,12... | collective-permute-start | bytes 3145736 | tf_op jit(solution)/shard_map/ppermute | solution.py:219
  121.1 19.5 %collective-permute-done.20.dn0 = bf16[256,2048]{1,0:T(8,128)(2,1)S(1)} collective-permute-done((bf16[256,2048]{1,0:T(8,128)(2,1)S(1)}, bf16[256,2048]{1,0:T(8,128)(2,1)S(1)}, u32[]{:S(2)}, u32[]{:S(2)}) %collective-permute-start.20) | collective-permute-done | bytes 1048608 | tf_op jit(solution)/shard_map/ppermute | solution.py:219
  146.6 12.0 %shard_map.113 = bf16[512,2304]{1,0:T(8,128)(2,1)} custom-call(bf16[512,2304]{1,0:T(8,128)(2,1)} %bitcast.37, bf16[2,2048,256]{2,1,0:T(8,128)(2,1)} %collective-permute-done.16.gu0, bf16[2,2048,256]{2,1,0:T(8,128)(2,1)} %collective-permute-done.17.gu1, bf16[2,2048,256]{2,1,0:T(8,128)(2,1)} %collective-permute-done.18.gu2, ...), custom_call_target="tpu_custom_call" | custom-call | tf_op jit(solution)/shard_map/pallas_call | solution.py:337
  158.6 9.0 %all-to-all-start.1 = ((bf16[32,16,2304]{2,1,0:T(8,128)(2,1)}), bf16[32,16,2304]{2,1,0:T(8,128)(2,1)S(1)}, u32[]{:S(2)}, u32[]{:S(2)}) async-start(bf16[32,16,2304]{2,1,0:T(8,128)(2,1)} %bitcast.38), calls=%async_computation.1 | async-start | bytes 4718592 | tf_op jit(solution)/shard_map/all_to_all | solution.py:351
  168.7 30.1 %all-to-all-done.1 = bf16[32,16,2304]{2,1,0:T(8,128)(2,1)S(1)} async-done(((bf16[32,16,2304]{2,1,0:T(8,128)(2,1)}), bf16[32,16,2304]{2,1,0:T(8,128)(2,1)S(1)}, u32[]{:S(2)}, u32[]{:S(2)}) %all-to-all-start.1) | async-done | bytes 2359328 | tf_op jit(solution)/shard_map/all_to_all | solution.py:351
  200.3 4.7 %shard_map.114 = (f32[64,2048]{1,0:T(8,128)}, bf16[64,2048]{1,0:T(8,128)(2,1)}, bf16[64,2048]{1,0:T(8,128)(2,1)}, bf16[64,2048]{1,0:T(8,128)(2,1)}) custom-call(bf16[512,576]{1,0:T(8,128)(2,1)} %pad_maximum_fusion.weight_ref, bf16[512,2304]{1,0:T(8,128)(2,1)} %bitcast.36), custom_call_target="tpu_custom_call" | custom-call | tf_op jit(solution)/shard_map/pallas_call | solution.py:352
  207.1 5.0 %collective-permute-done.26 = bf16[64,2048]{1,0:T(8,128)(2,1)S(1)} collective-permute-done((bf16[64,2048]{1,0:T(8,128)(2,1)}, bf16[64,2048]{1,0:T(8,128)(2,1)S(1)}, u32[]{:S(2)}, u32[]{:S(2)}) %collective-permute-start.26) | collective-permute-done | bytes 262176 | tf_op jit(solution)/shard_map/ppermute | solution.py:252
  212.2 2.9 %collective-permute-done.25 = bf16[64,2048]{1,0:T(8,128)(2,1)S(1)} collective-permute-done((bf16[64,2048]{1,0:T(8,128)(2,1)}, bf16[64,2048]{1,0:T(8,128)(2,1)S(1)}, u32[]{:S(2)}, u32[]{:S(2)}) %collective-permute-start.25) | collective-permute-done | bytes 262176 | tf_op jit(solution)/shard_map/ppermute | solution.py:252
  215.1 6.4 %collective-permute-done.24 = bf16[64,2048]{1,0:T(8,128)(2,1)S(1)} collective-permute-done((bf16[64,2048]{1,0:T(8,128)(2,1)}, bf16[64,2048]{1,0:T(8,128)(2,1)S(1)}, u32[]{:S(2)}, u32[]{:S(2)}) %collective-permute-start.24) | collective-permute-done | bytes 262176 | tf_op jit(solution)/shard_map/ppermute | solution.py:252
  (114 shorter events, 51.8 us)
Async XLA Ops:
  1.4 28.3 %collective-permute-start.12 = (f32[64,16]{0,1:T(8,128)S(1)}, f32[64,16]{0,1:T(8,128)S(1)}, u32[]{:S(2)}, u32[]{:S(2)}) collective-permute-start(f32[64,16]{0,1:T(8,128)S(1)} %pad_maximum_fusion.2), channel_id=1, source_target_pairs={{0,3},{1,0},{2,1},{3,2},{4,7},{5,4},{6,5},{7,6},{8,11},{9,8},{10,9... | collective-permute-start | bytes 12296 | tf_op jit(solution)/shard_map/ppermute | solution.py:246
  4.7 28.5 %collective-permute-start.11 = (f32[64,16]{0,1:T(8,128)S(1)}, f32[64,16]{0,1:T(8,128)S(1)}, u32[]{:S(2)}, u32[]{:S(2)}) collective-permute-start(f32[64,16]{0,1:T(8,128)S(1)} %pad_maximum_fusion.2), channel_id=1, source_target_pairs={{0,2},{1,3},{2,0},{3,1},{4,6},{5,7},{6,4},{7,5},{8,10},{9,11},{10,... | collective-permute-start | bytes 12296 | tf_op jit(solution)/shard_map/ppermute | solution.py:246
  5.2 28.0 %collective-permute-start.10 = (f32[64,16]{0,1:T(8,128)S(1)}, f32[64,16]{0,1:T(8,128)S(1)}, u32[]{:S(2)}, u32[]{:S(2)}) collective-permute-start(f32[64,16]{0,1:T(8,128)S(1)} %pad_maximum_fusion.2), channel_id=1, source_target_pairs={{0,1},{1,2},{2,3},{3,0},{4,5},{5,6},{6,7},{7,4},{8,9},{9,10},{10,1... | collective-permute-start | bytes 12296 | tf_op jit(solution)/shard_map/ppermute | solution.py:246
  16.6 16.7 %collective-permute-start = (bf16[4,128,128]{2,1,0:T(8,128)(2,1)}, bf16[4,128,128]{2,1,0:T(8,128)(2,1)S(1)}, u32[]{:S(2)}, u32[]{:S(2)}) collective-permute-start(bf16[4,128,128]{2,1,0:T(8,128)(2,1)} %get-tuple-element.20), channel_id=1, source_target_pairs={{0,4},{4,0},{8,12},{12,8},{16,20},{20,16},{24,28},{28,24},{32,36},... | collective-permute-start | bytes 393224 | tf_op jit(solution)/shard_map/ppermute | solution.py:281
  22.8 97.7 %collective-permute-start.16 = (bf16[2,2048,256]{2,1,0:T(8,128)(2,1)}, bf16[2,2048,256]{2,1,0:T(8,128)(2,1)}, u32[]{:S(2)}, u32[]{:S(2)}) collective-permute-start(bf16[2,2048,256]{2,1,0:T(8,128)(2,1)} %get-tuple-element.47), channel_id=1, source_target_pairs={{0,1},{1,4},{2,5},{3,0},{4,3},{5,6},{6,7},{7,2},{8,9},{9,12},{10,1... | collective-permute-start | bytes 6291464 | tf_op jit(solution)/shard_map/ppermute | solution.py:219
  29.7 90.9 %collective-permute-start.18 = (bf16[2,2048,256]{2,1,0:T(8,128)(2,1)}, bf16[2,2048,256]{2,1,0:T(8,128)(2,1)}, u32[]{:S(2)}, u32[]{:S(2)}) collective-permute-start(bf16[2,2048,256]{2,1,0:T(8,128)(2,1)} %get-tuple-element.46), channel_id=1, source_target_pairs={{0,0},{1,1},{2,4},{3,5},{4,2},{5,3},{6,6},{7,7},{8,8},{9,9},{10,12... | collective-permute-start | bytes 6291464 | tf_op jit(solution)/shard_map/ppermute | solution.py:219
  33.4 7.1 %collective-permute-start.3 = (bf16[4,128,128]{2,1,0:T(8,128)(2,1)S(1)}, bf16[4,128,128]{2,1,0:T(8,128)(2,1)S(1)}, u32[]{:S(2)}, u32[]{:S(2)}) collective-permute-start(bf16[4,128,128]{2,1,0:T(8,128)(2,1)S(1)} %fusion.10), channel_id=1, source_target_pairs={{0,24},{4,28},{8,0},{12,4},{16,8},{20,12},{24,16},{28,20},{32,56},... | collective-permute-start | bytes 393224 | tf_op jit(solution)/shard_map/ppermute | solution.py:242
  37.2 6.8 %collective-permute-start.1 = (bf16[4,128,128]{2,1,0:T(8,128)(2,1)S(1)}, bf16[4,128,128]{2,1,0:T(8,128)(2,1)S(1)}, u32[]{:S(2)}, u32[]{:S(2)}) collective-permute-start(bf16[4,128,128]{2,1,0:T(8,128)(2,1)S(1)} %fusion.10), channel_id=1, source_target_pairs={{0,8},{4,12},{8,16},{12,20},{16,24},{20,28},{24,0},{28,4},{32,40},... | collective-permute-start | bytes 393224 | tf_op jit(solution)/shard_map/ppermute | solution.py:242
  46.2 6.4 %collective-permute-start.5 = (bf16[4,128,128]{2,1,0:T(8,128)(2,1)S(1)}, bf16[4,128,128]{2,1,0:T(8,128)(2,1)S(1)}, u32[]{:S(2)}, u32[]{:S(2)}) collective-permute-start(bf16[4,128,128]{2,1,0:T(8,128)(2,1)S(1)} %get-tuple-element.50), channel_id=1, source_target_pairs={{0,64},{4,68},{8,72},{12,76},{16,80},{20,84},{24,88},{28,92},{32,9... | collective-permute-start | bytes 393224 | tf_op jit(solution)/shard_map/ppermute | solution.py:242
  57.9 21.3 %collective-permute-start.9 = (bf16[64,2048]{1,0:T(8,128)(2,1)}, bf16[64,2048]{1,0:T(8,128)(2,1)S(1)}, u32[]{:S(2)}, u32[]{:S(2)}) collective-permute-start(bf16[64,2048]{1,0:T(8,128)(2,1)} %get-tuple-element.30), channel_id=1, source_target_pairs={{0,3},{1,0},{2,1},{3,2},{4,7},{5,4},{6,5},{7,6},{8,11},{9,8},{10,9... | collective-permute-start | bytes 786440 | tf_op jit(solution)/shard_map/ppermute | solution.py:252
  71.7 7.6 %collective-permute-start.8 = (bf16[64,2048]{1,0:T(8,128)(2,1)}, bf16[64,2048]{1,0:T(8,128)(2,1)S(1)}, u32[]{:S(2)}, u32[]{:S(2)}) collective-permute-start(bf16[64,2048]{1,0:T(8,128)(2,1)} %get-tuple-element.29), channel_id=1, source_target_pairs={{0,2},{1,3},{2,0},{3,1},{4,6},{5,7},{6,4},{7,5},{8,10},{9,11},{10,... | collective-permute-start | bytes 786440 | tf_op jit(solution)/shard_map/ppermute | solution.py:252
  72.8 13.8 %collective-permute-start.7 = (bf16[64,2048]{1,0:T(8,128)(2,1)}, bf16[64,2048]{1,0:T(8,128)(2,1)S(1)}, u32[]{:S(2)}, u32[]{:S(2)}) collective-permute-start(bf16[64,2048]{1,0:T(8,128)(2,1)} %get-tuple-element.28), channel_id=1, source_target_pairs={{0,1},{1,2},{2,3},{3,0},{4,5},{5,6},{6,7},{7,4},{8,9},{9,10},{10,1... | collective-permute-start | bytes 786440 | tf_op jit(solution)/shard_map/ppermute | solution.py:252
  88.1 9.3 %collective-permute-start.13 = (bf16[64,2048]{1,0:T(8,128)(2,1)S(1)}, bf16[64,2048]{1,0:T(8,128)(2,1)S(1)}, u32[]{:S(2)}, u32[]{:S(2)}) collective-permute-start(bf16[64,2048]{1,0:T(8,128)(2,1)S(1)} %multiply_convert_fusion.t0), channel_id=1, source_target_pairs={{0,1},{1,2},{2,3},{3,0},{4,5},{5,6},{6,7},{7,4},{8,9},{9,10},{10,1... | collective-permute-start | bytes 786440 | tf_op jit(solution)/shard_map/ppermute | solution.py:246
  88.2 12.2 %collective-permute-start.14 = (bf16[64,2048]{1,0:T(8,128)(2,1)S(1)}, bf16[64,2048]{1,0:T(8,128)(2,1)S(1)}, u32[]{:S(2)}, u32[]{:S(2)}) collective-permute-start(bf16[64,2048]{1,0:T(8,128)(2,1)S(1)} %multiply_convert_fusion.t0), channel_id=1, source_target_pairs={{0,2},{1,3},{2,0},{3,1},{4,6},{5,7},{6,4},{7,5},{8,10},{9,11},{10,... | collective-permute-start | bytes 786440 | tf_op jit(solution)/shard_map/ppermute | solution.py:246
  89.7 13.1 %collective-permute-start.15 = (bf16[64,2048]{1,0:T(8,128)(2,1)S(1)}, bf16[64,2048]{1,0:T(8,128)(2,1)S(1)}, u32[]{:S(2)}, u32[]{:S(2)}) collective-permute-start(bf16[64,2048]{1,0:T(8,128)(2,1)S(1)} %multiply_convert_fusion.t0), channel_id=1, source_target_pairs={{0,3},{1,0},{2,1},{3,2},{4,7},{5,4},{6,5},{7,6},{8,11},{9,8},{10,9... | collective-permute-start | bytes 786440 | tf_op jit(solution)/shard_map/ppermute | solution.py:246
  107.0 38.2 %all-to-all-start = ((bf16[32,16,2304]{2,1,0:T(8,128)(2,1)}), bf16[32,16,2304]{2,1,0:T(8,128)(2,1)S(1)}, u32[]{:S(2)}, u32[]{:S(2)}) async-start(bf16[32,16,2304]{2,1,0:T(8,128)(2,1)} %bitcast.35), calls=%async_computation | async-start | bytes 4718592 | tf_op jit(solution)/shard_map/all_to_all | solution.py:336
  115.2 25.4 %collective-permute-start.20 = (bf16[256,2048]{1,0:T(8,128)(2,1)S(1)}, bf16[256,2048]{1,0:T(8,128)(2,1)S(1)}, u32[]{:S(2)}, u32[]{:S(2)}) collective-permute-start(bf16[256,2048]{1,0:T(8,128)(2,1)S(1)} %get-tuple-element.49), channel_id=1, source_target_pairs={{0,1},{1,4},{2,5},{3,0},{4,3},{5,6},{6,7},{7,2},{8,9},{9,12},{10,1... | collective-permute-start | bytes 3145736 | tf_op jit(solution)/shard_map/ppermute | solution.py:219
  117.6 24.8 %collective-permute-start.22 = (bf16[256,2048]{1,0:T(8,128)(2,1)S(1)}, bf16[256,2048]{1,0:T(8,128)(2,1)S(1)}, u32[]{:S(2)}, u32[]{:S(2)}) collective-permute-start(bf16[256,2048]{1,0:T(8,128)(2,1)S(1)} %get-tuple-element.48), channel_id=1, source_target_pairs={{0,0},{1,1},{2,4},{3,5},{4,2},{5,3},{6,6},{7,7},{8,8},{9,9},{10,12... | collective-permute-start | bytes 3145736 | tf_op jit(solution)/shard_map/ppermute | solution.py:219
  120.5 24.7 %collective-permute-start.17 = (bf16[2,2048,256]{2,1,0:T(8,128)(2,1)}, bf16[2,2048,256]{2,1,0:T(8,128)(2,1)}, u32[]{:S(2)}, u32[]{:S(2)}) collective-permute-start(bf16[2,2048,256]{2,1,0:T(8,128)(2,1)} %collective-permute-done.16.gu0), channel_id=1, source_target_pairs={{0,4},{4,0},{8,12},{12,8},{16,20},{20,16},{24,28},{28,24},{32,36},... | collective-permute-start | bytes 6291464 | tf_op jit(solution)/shard_map/ppermute | solution.py:219
  120.6 24.6 %collective-permute-start.19 = (bf16[2,2048,256]{2,1,0:T(8,128)(2,1)}, bf16[2,2048,256]{2,1,0:T(8,128)(2,1)}, u32[]{:S(2)}, u32[]{:S(2)}) collective-permute-start(bf16[2,2048,256]{2,1,0:T(8,128)(2,1)} %collective-permute-done.18.gu2), channel_id=1, source_target_pairs={{0,4},{4,0},{8,12},{12,8},{16,20},{20,16},{24,28},{28,24},{32,36},... | collective-permute-start | bytes 6291464 | tf_op jit(solution)/shard_map/ppermute | solution.py:219
  158.6 40.2 %all-to-all-start.1 = ((bf16[32,16,2304]{2,1,0:T(8,128)(2,1)}), bf16[32,16,2304]{2,1,0:T(8,128)(2,1)S(1)}, u32[]{:S(2)}, u32[]{:S(2)}) async-start(bf16[32,16,2304]{2,1,0:T(8,128)(2,1)} %bitcast.38), calls=%async_computation.1 | async-start | bytes 4718592 | tf_op jit(solution)/shard_map/all_to_all | solution.py:351
  204.9 7.2 %collective-permute-start.26 = (bf16[64,2048]{1,0:T(8,128)(2,1)}, bf16[64,2048]{1,0:T(8,128)(2,1)S(1)}, u32[]{:S(2)}, u32[]{:S(2)}) collective-permute-start(bf16[64,2048]{1,0:T(8,128)(2,1)} %get-tuple-element.34), channel_id=1, source_target_pairs={{0,3},{1,0},{2,1},{3,2},{4,7},{5,4},{6,5},{7,6},{8,11},{9,8},{10,9... | collective-permute-start | bytes 786440 | tf_op jit(solution)/shard_map/ppermute | solution.py:252
  206.6 8.6 %collective-permute-start.25 = (bf16[64,2048]{1,0:T(8,128)(2,1)}, bf16[64,2048]{1,0:T(8,128)(2,1)S(1)}, u32[]{:S(2)}, u32[]{:S(2)}) collective-permute-start(bf16[64,2048]{1,0:T(8,128)(2,1)} %get-tuple-element.33), channel_id=1, source_target_pairs={{0,2},{1,3},{2,0},{3,1},{4,6},{5,7},{6,4},{7,5},{8,10},{9,11},{10,... | collective-permute-start | bytes 786440 | tf_op jit(solution)/shard_map/ppermute | solution.py:252
  206.6 15.0 %collective-permute-start.24 = (bf16[64,2048]{1,0:T(8,128)(2,1)}, bf16[64,2048]{1,0:T(8,128)(2,1)S(1)}, u32[]{:S(2)}, u32[]{:S(2)}) collective-permute-start(bf16[64,2048]{1,0:T(8,128)(2,1)} %get-tuple-element.32), channel_id=1, source_target_pairs={{0,1},{1,2},{2,3},{3,0},{4,5},{5,6},{6,7},{7,4},{8,9},{9,10},{10,1... | collective-permute-start | bytes 786440 | tf_op jit(solution)/shard_map/ppermute | solution.py:252
  (21 other events, 112.8 us)
where the time goes:
time: 225 us; the launch traced here: 223 us
  waiting for transfers between devices  98.6 us (44%)
  starting transfers between devices  63.8 us (28%)
  Pallas kernels  33.6 us (15%)
  local copies, waits for them, and re-layouts  19.1 us (8%)
  other arithmetic  7.71 us (3%)
    all_to_all x1, waiting for transfers between devices, on_device(): lax.all_to_all(results.reshape(32, 16, PACKED), 'seq', 0, 0, tiled=True)  30.1 us
    ppermute x6, waiting for transfers between devices, scatter_head(): total = total + lax.ppermute(blocks[k], 'head', head_perm(k)).astype(F32)  27.3 us
    ppermute x8, waiting for transfers between devices, permute_all(): return [lax.ppermute(a, axes, perm) for a in arrays]  23 us
    ppermute x6, starting transfers between devices, scatter_head(): total = total + lax.ppermute(blocks[k], 'head', head_perm(k)).astype(F32)  17.8 us
    pallas_call x1, Pallas kernels, on_device(): call(expert_kernel, [ANY] * 9, [out((MAIN, PACKED), BF)], [pltpu.VMEM((SL...  12 us
    ppermute x8, starting transfers between devices, permute_all(): return [lax.ppermute(a, axes, perm) for a in arrays]  11.3 us
    ppermute x6, waiting for transfers between devices, gather_head(): lax.ppermute(array, 'head', head_perm(k))  10.2 us
    ppermute x6, starting transfers between devices, exchange(): lax.ppermute(array, 'seq', seq_perm(dy * k, dz * k, 0))  9.51 us
  transfers between devices with their start and end apart: 29, of which 18 were waited for; matrix products, arithmetic and copies ran while one was open for 8% of the time, Pallas kernels for 8%

commit v1 on v0

--- a/solution.py
+++ b/solution.py
@@ -134,16 +134,37 @@
         out_ref[:, D + t * 128:D + (t + 1) * 128] = piece
 
 
-def expert_kernel(x_ref, gu0, gu1, gu2, gu3, dn0, dn1, dn2, dn3, out_ref, rows, ends, gate_up, down, act, tail, sems):
+def expert_kernel(
+    keep_ref, x_ref, gu0, gu1, gu2, gu3, gu4, gu5, dn0, dn1, dn2, dn3, dn4, dn5,
+    out_ref, rows, ends, gate_up, down, act, tail, sems,
+):
     copies = [
         pltpu.make_async_copy(x_ref.at[:, :D], rows.at[:MAIN], sems.at[8]),
         pltpu.make_async_copy(x_ref.at[:, D:], ends, sems.at[9]),
     ]
-    for q, (gu, dn) in enumerate(((gu0, dn0), (gu1, dn1), (gu2, dn2), (gu3, dn3))):
-        copies.append(pltpu.make_async_copy(gu, gate_up.at[q], sems.at[q]))
-        copies.append(pltpu.make_async_copy(dn, down.at[q * 256:(q + 1) * 256], sems.at[4 + q]))
+
+    def load(q, gu, dn):
+        return [
+            pltpu.make_async_copy(gu, gate_up.at[q], sems.at[q]),
+            pltpu.make_async_copy(dn, down.at[q * 256:(q + 1) * 256], sems.at[4 + q]),
+        ]
+
+    copies += load(0, gu0, dn0) + load(1, gu1, dn1)
     for copy in copies:
         copy.start()
+    keep = keep_ref[0] == 1
+
+    @pl.when(keep)
+    def _():
+        for copy in load(2, gu2, dn2) + load(3, gu5, dn5):
+            copy.start()
+
+    @pl.when(jnp.logical_not(keep))
+    def _():
+        for copy in load(2, gu3, dn3) + load(3, gu4, dn4):
+            copy.start()
+
+    copies += load(2, gu2, dn2) + load(3, gu4, dn4)
     copies[1].wait()
     for t in range(2):
         piece = ends[:, t * 128:(t + 1) * 128].astype(F32).reshape(32, D)
@@ -202,6 +223,8 @@
         for c in range(2):
             for h in range(4):
                 to = target(c, h)
+                if to is None:
+                    continue
                 pairs.append(((chip * 2 + c) * 4 + h, (chip * 2 + to[0]) * 4 + to[1]))
     return pairs
 
@@ -212,7 +235,15 @@
 
 
 def far_target(c, h):
-    return (c, h) if h // 2 == c else (1 - c, (h + 2) % 4)
+    return None if h // 2 == c else (1 - c, (h + 2) % 4)
+
+
+def keep_target(c, h):
+    return (1 - c, h) if h // 2 == c else None
+
+
+def pass_target(c, h):
+    return None if h // 2 == c else (1 - c, h)
 
 
 def permute_all(arrays, axes, perm):
@@ -231,10 +262,12 @@
     both = ("seq", "head")
     swap = seq_perm(0, 0, 1)
     near = permute_all(pick(1 - odd), both, device_perm(near_target))
-    far = permute_all(pick(odd), both, device_perm(far_target))
+    rest = pick(odd)
+    far = permute_all(rest, both, device_perm(far_target))
+    rest_other = permute_all(rest, both, device_perm(keep_target))
     near_other = permute_all(near, "seq", swap)
-    far_other = permute_all(far, "seq", swap)
-    return [near, near_other, far, far_other]
+    far_other = permute_all(far, both, device_perm(pass_target))
+    return [near, near_other, rest, rest_other, far, far_other]
 
 
 def exchange(array, step):
@@ -334,9 +367,10 @@
         dispatch_kernel, [VMEM] * 5, [out((MAIN, PACKED), BF)], [pltpu.VMEM((TOK, D), BF)]
     )(place_rows.astype(BF), *tokens)[0]
     received = lax.all_to_all(sent.reshape(32, 16, PACKED), "seq", 0, 0, tiled=True)
+    keep = (head // 2 == core).astype(jnp.int32)[None]
     results = call(
         expert_kernel,
-        [ANY] * 9,
+        [SMEM] + [ANY] * 13,
         [out((MAIN, PACKED), BF)],
         [
             pltpu.VMEM((SLOTS, D), BF),
@@ -347,7 +381,7 @@
             pltpu.VMEM((64, D), F32),
             pltpu.SemaphoreType.DMA((10,)),
         ],
-    )(received.reshape(MAIN, PACKED), *[p[0] for p in pieces], *[p[1] for p in pieces])[0]
+    )(keep, received.reshape(MAIN, PACKED), *[p[0] for p in pieces], *[p[1] for p in pieces])[0]
     back = lax.all_to_all(results.reshape(32, 16, PACKED), "seq", 0, 0, tiled=True)
     blocks = call(
         combine_kernel, [VMEM] * 2, BLOCKS_OUT, [pltpu.VMEM((64, D), BF)]

time: 225 us -> 242 us (1.076)
  the two profiles are of different devices: /device:TPU:1 before, /device:TPU:33 now
where the time goes in v1:
time: 242 us; the launch traced here: 238 us
  waiting for transfers between devices  108 us (45%)
  starting transfers between devices  70 us (29%)
  Pallas kernels  33.6 us (14%)
  local copies, waits for them, and re-layouts  18 us (7%)
  other arithmetic  7.52 us (3%)
    ppermute x6, waiting for transfers between devices, scatter_head(): total = total + lax.ppermute(blocks[k], 'head', head_perm(k)).astype(F32)  50.3 us
    all_to_all x1, waiting for transfers between devices, on_device(): lax.all_to_all(results.reshape(32, 16, PACKED), 'seq', 0, 0, tiled=True)  28.5 us
    ppermute x6, starting transfers between devices, gather_head(): lax.ppermute(array, 'head', head_perm(k))  21.7 us
    ppermute x10, starting transfers between devices, permute_all(): return [lax.ppermute(a, axes, perm) for a in arrays]  18.7 us
    pallas_call x1, Pallas kernels, on_device(): call(expert_kernel, [SMEM] + [ANY] * 13, [out((MAIN, PACKED), BF)], [pltp...  12 us
    ppermute x10, waiting for transfers between devices, permute_all(): return [lax.ppermute(a, axes, perm) for a in arrays]  11.3 us
    ppermute x6, starting transfers between devices, exchange(): lax.ppermute(array, 'seq', seq_perm(dy * k, dz * k, 0))  9.82 us
    ppermute x6, waiting for transfers between devices, gather_head(): lax.ppermute(array, 'head', head_perm(k))  8.63 us
  transfers between devices with their start and end apart: 31, of which 13 were waited for; matrix products, arithmetic and copies ran while one was open for 8% of the time, Pallas kernels for 7%

profile of v1, /device:TPU:33, one launch (start us, length us, event | category | flops | bytes accessed | tf_op | source)
XLA Modules:
  0.0 238.2 jit_solution(13532369440818260544)
XLA Ops:
  5.0 5.6 %slice_bitcast_fusion = (bf16[2048,512]{1,0:T(8,128)(2,1)}, bf16[2048,512]{1,0:T(8,128)(2,1)}, bf16[2048,512]{1,0:T(8,128)(2,1)}) fusion(bf16[2048,3,512]{2,0,1:T(8,128)(2,1)} %param.13), kind=kLoop, calls=%fused_computation.2 | loop fusion | bytes 12582912 | tf_op jit(solution)/shard_map/squeeze | solution.py:325
  10.6 5.2 %shard_map.109 = (bf16[256,2048]{1,0:T(8,128)(2,1)}, bf16[256,512]{1,0:T(8,128)(2,1)}, bf16[256,512]{1,0:T(8,128)(2,1)}, f32[4,128,128]{2,1,0:T(8,128)}, bf16[4,128,128]{2,1,0:T(8,128)(2,1)}) custom-call(bf16[256,2048]{1,0:T(8,128)(2,1)} %x_ref.1, f32[1,2048]{1,0:T(1,128)} %bitcast.44, bf16[2048,512]{1,0:T(8,128)(2,1)} %get-tuple-element.44.wk_ref, ...), custom_call_target="tpu_custom_call" | custom-call | tf_op jit(solution)/shard_map/pallas_call | solution.py:302
  17.5 4.6 %dynamic-slice_bitcast_fusion = (bf16[2,2048,256]{2,1,0:T(8,128)(2,1)}, bf16[2,2048,256]{2,1,0:T(8,128)(2,1)}) fusion(bf16[2,2,2048,256]{3,2,1,0:T(8,128)(2,1)} %param.19, s32[]{:T(128)S(6)} %select_n.145, s32[]{:T(128)S(6)} %select_n.144), kind=kLoop, calls=%fused_computation | loop fusion | bytes 8388616 | tf_op jit(solution)/shard_map/jit(dynamic_index_in_dim)/squeeze | solution.py:258
  23.9 2.8 %collective-permute-start.2 = (bf16[4,128,128]{2,1,0:T(8,128)(2,1)S(1)}, bf16[4,128,128]{2,1,0:T(8,128)(2,1)S(1)}, u32[]{:S(2)}, u32[]{:S(2)}) collective-permute-start(bf16[4,128,128]{2,1,0:T(8,128)(2,1)S(1)} %fusion.10), channel_id=1, source_target_pairs={{0,16},{4,20},{8,24},{12,28},{16,0},{20,4},{24,8},{28,12},{32,48},... | collective-permute-start | bytes 393224 | tf_op jit(solution)/shard_map/ppermute | solution.py:275
  29.4 3.9 %shard_map.110 = (bf16[256,512]{1,0:T(8,128)(2,1)}, f32[256,512]{1,0:T(8,128)}) custom-call(bf16[256,2048]{1,0:T(8,128)(2,1)} %get-tuple-element.22.normed_ref, bf16[2048,512]{1,0:T(8,128)(2,1)} %get-tuple-element.43.wq_ref, bf16[256,512]{1,0:T(8,128)(2,1)} %get-tuple-element.23.k_ref, bf16[256,512]{1,0:T(8,128)(2,1)} %get-tuple-element.24.v_ref), custom_call_target="tpu_custom_call" | custom-call | tf_op jit(solution)/shard_map/pallas_call | solution.py:323
  33.4 2.8 %collective-permute-start.16 = (bf16[2,2048,256]{2,1,0:T(8,128)(2,1)}, bf16[2,2048,256]{2,1,0:T(8,128)(2,1)}, u32[]{:S(2)}, u32[]{:S(2)}) collective-permute-start(bf16[2,2048,256]{2,1,0:T(8,128)(2,1)} %get-tuple-element.47), channel_id=1, source_target_pairs={{0,1},{1,4},{2,5},{3,0},{4,3},{5,6},{6,7},{7,2},{8,9},{9,12},{10,1... | collective-permute-start | bytes 6291464 | tf_op jit(solution)/shard_map/ppermute | solution.py:250
  46.3 3.6 %collective-permute-done.5.g2 = bf16[4,128,128]{2,1,0:T(8,128)(2,1)S(1)} collective-permute-done((bf16[4,128,128]{2,1,0:T(8,128)(2,1)S(1)}, bf16[4,128,128]{2,1,0:T(8,128)(2,1)S(1)}, u32[]{:S(2)}, u32[]{:S(2)}) %collective-permute-start.5) | collective-permute-done | bytes 131104 | tf_op jit(solution)/shard_map/ppermute | solution.py:275
  50.6 4.3 %shard_map.111 = (f32[64,2048]{1,0:T(8,128)}, bf16[64,2048]{1,0:T(8,128)(2,1)}, bf16[64,2048]{1,0:T(8,128)(2,1)}, bf16[64,2048]{1,0:T(8,128)(2,1)}) custom-call(s32[2]{0:T(128)} %pad_add_fusion.place_ref, f32[4,128,128]{2,1,0:T(8,128)} %get-tuple-element.51.prefix_ref, bf16[4,128,128]{2,1,0:T(8,128)(2,1)} %copy-done.9, bf16[4,128,128]{2,1,0:T(8,128)(2,1)} %copy-done.10, ...), custom_call_target="tpu_custom_call" | custom-call | tf_op jit(solution)/shard_map/pallas_call | solution.py:327
  57.7 35.5 %collective-permute-done.9 = bf16[64,2048]{1,0:T(8,128)(2,1)S(1)} collective-permute-done((bf16[64,2048]{1,0:T(8,128)(2,1)}, bf16[64,2048]{1,0:T(8,128)(2,1)S(1)}, u32[]{:S(2)}, u32[]{:S(2)}) %collective-permute-start.9) | collective-permute-done | bytes 262176 | tf_op jit(solution)/shard_map/ppermute | solution.py:285
  99.1 5.6 %collective-permute-done.13.t1 = bf16[64,2048]{1,0:T(8,128)(2,1)S(1)} collective-permute-done((bf16[64,2048]{1,0:T(8,128)(2,1)S(1)}, bf16[64,2048]{1,0:T(8,128)(2,1)S(1)}, u32[]{:S(2)}, u32[]{:S(2)}) %collective-permute-start.13) | collective-permute-done | bytes 262176 | tf_op jit(solution)/shard_map/ppermute | solution.py:279
  104.7 13.8 %collective-permute-start.15 = (bf16[64,2048]{1,0:T(8,128)(2,1)S(1)}, bf16[64,2048]{1,0:T(8,128)(2,1)S(1)}, u32[]{:S(2)}, u32[]{:S(2)}) collective-permute-start(bf16[64,2048]{1,0:T(8,128)(2,1)S(1)} %multiply_convert_fusion.t0), channel_id=1, source_target_pairs={{0,3},{1,0},{2,1},{3,2},{4,7},{5,4},{6,5},{7,6},{8,11},{9,8},{10,9... | collective-permute-start | bytes 786440 | tf_op jit(solution)/shard_map/ppermute | solution.py:279
  123.2 3.5 %shard_map.112 = bf16[512,2304]{1,0:T(8,128)(2,1)} custom-call(bf16[576,256]{1,0:T(8,128)(2,1)} %copy.33.place_ref, bf16[64,2048]{1,0:T(8,128)(2,1)} %copy-done.3, bf16[64,2048]{1,0:T(8,128)(2,1)} %copy-done.6, bf16[64,2048]{1,0:T(8,128)(2,1)} %copy-done.7, bf16[64,2048]{1,0:T(8,128)(2,1)} %copy-done.8), custom_call_target="tpu_custom_call" | custom-call | tf_op jit(solution)/shard_map/pallas_call | solution.py:366
  126.7 6.5 %all-to-all-start = ((bf16[32,16,2304]{2,1,0:T(8,128)(2,1)}), bf16[32,16,2304]{2,1,0:T(8,128)(2,1)S(1)}, u32[]{:S(2)}, u32[]{:S(2)}) async-start(bf16[32,16,2304]{2,1,0:T(8,128)(2,1)} %bitcast.38), calls=%async_computation | async-start | bytes 4718592 | tf_op jit(solution)/shard_map/all_to_all | solution.py:369
  135.9 3.5 %collective-permute-start.24 = (bf16[256,2048]{1,0:T(8,128)(2,1)}, bf16[256,2048]{1,0:T(8,128)(2,1)}, u32[]{:S(2)}, u32[]{:S(2)}) collective-permute-start(bf16[256,2048]{1,0:T(8,128)(2,1)} %get-tuple-element.48.dn2), channel_id=1, source_target_pairs={{2,4},{3,5},{4,2},{5,3},{10,12},{11,13},{12,10},{13,11},{18,20},{1... | collective-permute-start | bytes 3145736 | tf_op jit(solution)/shard_map/ppermute | solution.py:250
  141.1 3.2 %collective-permute-start.20 = (bf16[2,2048,256]{2,1,0:T(8,128)(2,1)}, bf16[2,2048,256]{2,1,0:T(8,128)(2,1)}, u32[]{:S(2)}, u32[]{:S(2)}) collective-permute-start(bf16[2,2048,256]{2,1,0:T(8,128)(2,1)} %collective-permute-done.19.gu4), channel_id=1, source_target_pairs={{2,6},{3,7},{4,0},{5,1},{10,14},{11,15},{12,8},{13,9},{18,22},{19,... | collective-permute-start | bytes 6291464 | tf_op jit(solution)/shard_map/ppermute | solution.py:250
  144.3 9.7 %collective-permute-done.24.dn4 = bf16[256,2048]{1,0:T(8,128)(2,1)} collective-permute-done((bf16[256,2048]{1,0:T(8,128)(2,1)}, bf16[256,2048]{1,0:T(8,128)(2,1)}, u32[]{:S(2)}, u32[]{:S(2)}) %collective-permute-start.24) | collective-permute-done | bytes 1048608 | tf_op jit(solution)/shard_map/ppermute | solution.py:250
  157.9 4.6 %all-to-all-done = bf16[32,16,2304]{2,1,0:T(8,128)(2,1)S(1)} async-done(((bf16[32,16,2304]{2,1,0:T(8,128)(2,1)}), bf16[32,16,2304]{2,1,0:T(8,128)(2,1)S(1)}, u32[]{:S(2)}, u32[]{:S(2)}) %all-to-all-start) | async-done | bytes 2359328 | tf_op jit(solution)/shard_map/all_to_all | solution.py:369
  164.0 12.0 %shard_map.113 = bf16[512,2304]{1,0:T(8,128)(2,1)} custom-call(s32[1]{0:T(128)} %bitcast.12.keep_ref, bf16[512,2304]{1,0:T(8,128)(2,1)} %bitcast.36, bf16[2,2048,256]{2,1,0:T(8,128)(2,1)} %collective-permute-done.16.gu0, bf16[2,2048,256]{2,1,0:T(8,128)(2,1)} %collective-permute-done.17.gu1, bf16[2,2048,256]{2,1,0:T(8,128)(2,1)} %get-tuple-element.46.gu2, ...), custom_call_target="tpu_custom_call" | custom-call | tf_op jit(solution)/shard_map/pallas_call | solution.py:371
  176.0 6.5 %all-to-all-start.1 = ((bf16[32,16,2304]{2,1,0:T(8,128)(2,1)}), bf16[32,16,2304]{2,1,0:T(8,128)(2,1)S(1)}, u32[]{:S(2)}, u32[]{:S(2)}) async-start(bf16[32,16,2304]{2,1,0:T(8,128)(2,1)} %bitcast.37), calls=%async_computation.1 | async-start | bytes 4718592 | tf_op jit(solution)/shard_map/all_to_all | solution.py:385
  183.5 28.5 %all-to-all-done.1 = bf16[32,16,2304]{2,1,0:T(8,128)(2,1)S(1)} async-done(((bf16[32,16,2304]{2,1,0:T(8,128)(2,1)}), bf16[32,16,2304]{2,1,0:T(8,128)(2,1)S(1)}, u32[]{:S(2)}, u32[]{:S(2)}) %all-to-all-start.1) | async-done | bytes 2359328 | tf_op jit(solution)/shard_map/all_to_all | solution.py:385
  213.4 4.7 %shard_map.114 = (f32[64,2048]{1,0:T(8,128)}, bf16[64,2048]{1,0:T(8,128)(2,1)}, bf16[64,2048]{1,0:T(8,128)(2,1)}, bf16[64,2048]{1,0:T(8,128)(2,1)}) custom-call(bf16[512,576]{1,0:T(8,128)(2,1)} %pad_maximum_fusion.weight_ref, bf16[512,2304]{1,0:T(8,128)(2,1)} %bitcast.39), custom_call_target="tpu_custom_call" | custom-call | tf_op jit(solution)/shard_map/pallas_call | solution.py:386
  221.6 4.7 %collective-permute-done.28 = bf16[64,2048]{1,0:T(8,128)(2,1)S(1)} collective-permute-done((bf16[64,2048]{1,0:T(8,128)(2,1)}, bf16[64,2048]{1,0:T(8,128)(2,1)S(1)}, u32[]{:S(2)}, u32[]{:S(2)}) %collective-permute-start.28) | collective-permute-done | bytes 262176 | tf_op jit(solution)/shard_map/ppermute | solution.py:285
  226.3 2.9 %collective-permute-done.27 = bf16[64,2048]{1,0:T(8,128)(2,1)S(1)} collective-permute-done((bf16[64,2048]{1,0:T(8,128)(2,1)}, bf16[64,2048]{1,0:T(8,128)(2,1)S(1)}, u32[]{:S(2)}, u32[]{:S(2)}) %collective-permute-start.27) | collective-permute-done | bytes 262176 | tf_op jit(solution)/shard_map/ppermute | solution.py:285
  229.2 7.2 %collective-permute-done.26 = bf16[64,2048]{1,0:T(8,128)(2,1)S(1)} collective-permute-done((bf16[64,2048]{1,0:T(8,128)(2,1)}, bf16[64,2048]{1,0:T(8,128)(2,1)S(1)}, u32[]{:S(2)}, u32[]{:S(2)}) %collective-permute-start.26) | collective-permute-done | bytes 262176 | tf_op jit(solution)/shard_map/ppermute | solution.py:285
  (116 shorter events, 52.5 us)
Async XLA Ops:
  1.4 25.3 %collective-permute-start.12 = (f32[64,16]{0,1:T(8,128)S(1)}, f32[64,16]{0,1:T(8,128)S(1)}, u32[]{:S(2)}, u32[]{:S(2)}) collective-permute-start(f32[64,16]{0,1:T(8,128)S(1)} %pad_maximum_fusion.2), channel_id=1, source_target_pairs={{0,3},{1,0},{2,1},{3,2},{4,7},{5,4},{6,5},{7,6},{8,11},{9,8},{10,9... | collective-permute-start | bytes 12296 | tf_op jit(solution)/shard_map/ppermute | solution.py:279
  3.9 29.5 %collective-permute-start.11 = (f32[64,16]{0,1:T(8,128)S(1)}, f32[64,16]{0,1:T(8,128)S(1)}, u32[]{:S(2)}, u32[]{:S(2)}) collective-permute-start(f32[64,16]{0,1:T(8,128)S(1)} %pad_maximum_fusion.2), channel_id=1, source_target_pairs={{0,2},{1,3},{2,0},{3,1},{4,6},{5,7},{6,4},{7,5},{8,10},{9,11},{10,... | collective-permute-start | bytes 12296 | tf_op jit(solution)/shard_map/ppermute | solution.py:279
  4.4 31.8 %collective-permute-start.10 = (f32[64,16]{0,1:T(8,128)S(1)}, f32[64,16]{0,1:T(8,128)S(1)}, u32[]{:S(2)}, u32[]{:S(2)}) collective-permute-start(f32[64,16]{0,1:T(8,128)S(1)} %pad_maximum_fusion.2), channel_id=1, source_target_pairs={{0,1},{1,2},{2,3},{3,0},{4,5},{5,6},{6,7},{7,4},{8,9},{9,10},{10,1... | collective-permute-start | bytes 12296 | tf_op jit(solution)/shard_map/ppermute | solution.py:279
  23.8 15.2 %collective-permute-start.3 = (bf16[4,128,128]{2,1,0:T(8,128)(2,1)S(1)}, bf16[4,128,128]{2,1,0:T(8,128)(2,1)S(1)}, u32[]{:S(2)}, u32[]{:S(2)}) collective-permute-start(bf16[4,128,128]{2,1,0:T(8,128)(2,1)S(1)} %fusion.10), channel_id=1, source_target_pairs={{0,24},{4,28},{8,0},{12,4},{16,8},{20,12},{24,16},{28,20},{32,56},... | collective-permute-start | bytes 393224 | tf_op jit(solution)/shard_map/ppermute | solution.py:275
  23.9 15.1 %collective-permute-start.2 = (bf16[4,128,128]{2,1,0:T(8,128)(2,1)S(1)}, bf16[4,128,128]{2,1,0:T(8,128)(2,1)S(1)}, u32[]{:S(2)}, u32[]{:S(2)}) collective-permute-start(bf16[4,128,128]{2,1,0:T(8,128)(2,1)S(1)} %fusion.10), channel_id=1, source_target_pairs={{0,16},{4,20},{8,24},{12,28},{16,0},{20,4},{24,8},{28,12},{32,48},... | collective-permute-start | bytes 393224 | tf_op jit(solution)/shard_map/ppermute | solution.py:275
  26.7 12.3 %collective-permute-start.1 = (bf16[4,128,128]{2,1,0:T(8,128)(2,1)S(1)}, bf16[4,128,128]{2,1,0:T(8,128)(2,1)S(1)}, u32[]{:S(2)}, u32[]{:S(2)}) collective-permute-start(bf16[4,128,128]{2,1,0:T(8,128)(2,1)S(1)} %fusion.10), channel_id=1, source_target_pairs={{0,8},{4,12},{8,16},{12,20},{16,24},{20,28},{24,0},{28,4},{32,40},... | collective-permute-start | bytes 393224 | tf_op jit(solution)/shard_map/ppermute | solution.py:275
  33.4 106.0 %collective-permute-start.16 = (bf16[2,2048,256]{2,1,0:T(8,128)(2,1)}, bf16[2,2048,256]{2,1,0:T(8,128)(2,1)}, u32[]{:S(2)}, u32[]{:S(2)}) collective-permute-start(bf16[2,2048,256]{2,1,0:T(8,128)(2,1)} %get-tuple-element.47), channel_id=1, source_target_pairs={{0,1},{1,4},{2,5},{3,0},{4,3},{5,6},{6,7},{7,2},{8,9},{9,12},{10,1... | collective-permute-start | bytes 6291464 | tf_op jit(solution)/shard_map/ppermute | solution.py:250
  36.2 104.9 %collective-permute-start.19 = (bf16[2,2048,256]{2,1,0:T(8,128)(2,1)}, bf16[2,2048,256]{2,1,0:T(8,128)(2,1)}, u32[]{:S(2)}, u32[]{:S(2)}) collective-permute-start(bf16[2,2048,256]{2,1,0:T(8,128)(2,1)} %get-tuple-element.46.gu2), channel_id=1, source_target_pairs={{2,4},{3,5},{4,2},{5,3},{10,12},{11,13},{12,10},{13,11},{18,20},{1... | collective-permute-start | bytes 6291464 | tf_op jit(solution)/shard_map/ppermute | solution.py:250
  54.9 38.3 %collective-permute-start.9 = (bf16[64,2048]{1,0:T(8,128)(2,1)}, bf16[64,2048]{1,0:T(8,128)(2,1)S(1)}, u32[]{:S(2)}, u32[]{:S(2)}) collective-permute-start(bf16[64,2048]{1,0:T(8,128)(2,1)} %get-tuple-element.30), channel_id=1, source_target_pairs={{0,3},{1,0},{2,1},{3,2},{4,7},{5,4},{6,5},{7,6},{8,11},{9,8},{10,9... | collective-permute-start | bytes 786440 | tf_op jit(solution)/shard_map/ppermute | solution.py:285
  54.9 38.3 %collective-permute-start.8 = (bf16[64,2048]{1,0:T(8,128)(2,1)}, bf16[64,2048]{1,0:T(8,128)(2,1)S(1)}, u32[]{:S(2)}, u32[]{:S(2)}) collective-permute-start(bf16[64,2048]{1,0:T(8,128)(2,1)} %get-tuple-element.29), channel_id=1, source_target_pairs={{0,2},{1,3},{2,0},{3,1},{4,6},{5,7},{6,4},{7,5},{8,10},{9,11},{10,... | collective-permute-start | bytes 786440 | tf_op jit(solution)/shard_map/ppermute | solution.py:285
  56.5 36.8 %collective-permute-start.7 = (bf16[64,2048]{1,0:T(8,128)(2,1)}, bf16[64,2048]{1,0:T(8,128)(2,1)S(1)}, u32[]{:S(2)}, u32[]{:S(2)}) collective-permute-start(bf16[64,2048]{1,0:T(8,128)(2,1)} %get-tuple-element.28), channel_id=1, source_target_pairs={{0,1},{1,2},{2,3},{3,0},{4,5},{5,6},{6,7},{7,4},{8,9},{9,10},{10,1... | collective-permute-start | bytes 786440 | tf_op jit(solution)/shard_map/ppermute | solution.py:285
  93.2 42.6 %collective-permute-start.21 = (bf16[256,2048]{1,0:T(8,128)(2,1)}, bf16[256,2048]{1,0:T(8,128)(2,1)}, u32[]{:S(2)}, u32[]{:S(2)}) collective-permute-start(bf16[256,2048]{1,0:T(8,128)(2,1)} %get-tuple-element.49), channel_id=1, source_target_pairs={{0,1},{1,4},{2,5},{3,0},{4,3},{5,6},{6,7},{7,2},{8,9},{9,12},{10,1... | collective-permute-start | bytes 3145736 | tf_op jit(solution)/shard_map/ppermute | solution.py:250
  94.7 10.0 %collective-permute-start.13 = (bf16[64,2048]{1,0:T(8,128)(2,1)S(1)}, bf16[64,2048]{1,0:T(8,128)(2,1)S(1)}, u32[]{:S(2)}, u32[]{:S(2)}) collective-permute-start(bf16[64,2048]{1,0:T(8,128)(2,1)S(1)} %multiply_convert_fusion.t0), channel_id=1, source_target_pairs={{0,1},{1,2},{2,3},{3,0},{4,5},{5,6},{6,7},{7,4},{8,9},{9,10},{10,1... | collective-permute-start | bytes 786440 | tf_op jit(solution)/shard_map/ppermute | solution.py:279
  96.7 24.4 %collective-permute-start.14 = (bf16[64,2048]{1,0:T(8,128)(2,1)S(1)}, bf16[64,2048]{1,0:T(8,128)(2,1)S(1)}, u32[]{:S(2)}, u32[]{:S(2)}) collective-permute-start(bf16[64,2048]{1,0:T(8,128)(2,1)S(1)} %multiply_convert_fusion.t0), channel_id=1, source_target_pairs={{0,2},{1,3},{2,0},{3,1},{4,6},{5,7},{6,4},{7,5},{8,10},{9,11},{10,... | collective-permute-start | bytes 786440 | tf_op jit(solution)/shard_map/ppermute | solution.py:279
  104.7 17.8 %collective-permute-start.15 = (bf16[64,2048]{1,0:T(8,128)(2,1)S(1)}, bf16[64,2048]{1,0:T(8,128)(2,1)S(1)}, u32[]{:S(2)}, u32[]{:S(2)}) collective-permute-start(bf16[64,2048]{1,0:T(8,128)(2,1)S(1)} %multiply_convert_fusion.t0), channel_id=1, source_target_pairs={{0,3},{1,0},{2,1},{3,2},{4,7},{5,4},{6,5},{7,6},{8,11},{9,8},{10,9... | collective-permute-start | bytes 786440 | tf_op jit(solution)/shard_map/ppermute | solution.py:279
  126.7 35.8 %all-to-all-start = ((bf16[32,16,2304]{2,1,0:T(8,128)(2,1)}), bf16[32,16,2304]{2,1,0:T(8,128)(2,1)S(1)}, u32[]{:S(2)}, u32[]{:S(2)}) async-start(bf16[32,16,2304]{2,1,0:T(8,128)(2,1)} %bitcast.38), calls=%async_computation | async-start | bytes 4718592 | tf_op jit(solution)/shard_map/all_to_all | solution.py:369
  133.3 23.0 %collective-permute-start.18 = (bf16[2,2048,256]{2,1,0:T(8,128)(2,1)}, bf16[2,2048,256]{2,1,0:T(8,128)(2,1)}, u32[]{:S(2)}, u32[]{:S(2)}) collective-permute-start(bf16[2,2048,256]{2,1,0:T(8,128)(2,1)} %get-tuple-element.46.gu2), channel_id=1, source_target_pairs={{0,4},{1,5},{6,2},{7,3},{8,12},{9,13},{14,10},{15,11},{16,20},{17,... | collective-permute-start | bytes 6291464 | tf_op jit(solution)/shard_map/ppermute | solution.py:250
  134.6 9.7 %collective-permute-start.23 = (bf16[256,2048]{1,0:T(8,128)(2,1)}, bf16[256,2048]{1,0:T(8,128)(2,1)}, u32[]{:S(2)}, u32[]{:S(2)}) collective-permute-start(bf16[256,2048]{1,0:T(8,128)(2,1)} %get-tuple-element.48.dn2), channel_id=1, source_target_pairs={{0,4},{1,5},{6,2},{7,3},{8,12},{9,13},{14,10},{15,11},{16,20},{17,... | collective-permute-start | bytes 3145736 | tf_op jit(solution)/shard_map/ppermute | solution.py:250
  135.9 18.1 %collective-permute-start.24 = (bf16[256,2048]{1,0:T(8,128)(2,1)}, bf16[256,2048]{1,0:T(8,128)(2,1)}, u32[]{:S(2)}, u32[]{:S(2)}) collective-permute-start(bf16[256,2048]{1,0:T(8,128)(2,1)} %get-tuple-element.48.dn2), channel_id=1, source_target_pairs={{2,4},{3,5},{4,2},{5,3},{10,12},{11,13},{12,10},{13,11},{18,20},{1... | collective-permute-start | bytes 3145736 | tf_op jit(solution)/shard_map/ppermute | solution.py:250
  139.4 23.1 %collective-permute-start.17 = (bf16[2,2048,256]{2,1,0:T(8,128)(2,1)}, bf16[2,2048,256]{2,1,0:T(8,128)(2,1)}, u32[]{:S(2)}, u32[]{:S(2)}) collective-permute-start(bf16[2,2048,256]{2,1,0:T(8,128)(2,1)} %collective-permute-done.16.gu0), channel_id=1, source_target_pairs={{0,4},{4,0},{8,12},{12,8},{16,20},{20,16},{24,28},{28,24},{32,36},... | collective-permute-start | bytes 6291464 | tf_op jit(solution)/shard_map/ppermute | solution.py:250
  141.1 21.5 %collective-permute-start.20 = (bf16[2,2048,256]{2,1,0:T(8,128)(2,1)}, bf16[2,2048,256]{2,1,0:T(8,128)(2,1)}, u32[]{:S(2)}, u32[]{:S(2)}) collective-permute-start(bf16[2,2048,256]{2,1,0:T(8,128)(2,1)} %collective-permute-done.19.gu4), channel_id=1, source_target_pairs={{2,6},{3,7},{4,0},{5,1},{10,14},{11,15},{12,8},{13,9},{18,22},{19,... | collective-permute-start | bytes 6291464 | tf_op jit(solution)/shard_map/ppermute | solution.py:250
  144.3 12.0 %collective-permute-start.22 = (bf16[256,2048]{1,0:T(8,128)(2,1)}, bf16[256,2048]{1,0:T(8,128)(2,1)}, u32[]{:S(2)}, u32[]{:S(2)}) collective-permute-start(bf16[256,2048]{1,0:T(8,128)(2,1)} %collective-permute-done.21.dn0), channel_id=1, source_target_pairs={{0,4},{4,0},{8,12},{12,8},{16,20},{20,16},{24,28},{28,24},{32,36},... | collective-permute-start | bytes 3145736 | tf_op jit(solution)/shard_map/ppermute | solution.py:250
  176.0 36.0 %all-to-all-start.1 = ((bf16[32,16,2304]{2,1,0:T(8,128)(2,1)}), bf16[32,16,2304]{2,1,0:T(8,128)(2,1)S(1)}, u32[]{:S(2)}, u32[]{:S(2)}) async-start(bf16[32,16,2304]{2,1,0:T(8,128)(2,1)} %bitcast.37), calls=%async_computation.1 | async-start | bytes 4718592 | tf_op jit(solution)/shard_map/all_to_all | solution.py:385
  221.6 14.7 %collective-permute-start.26 = (bf16[64,2048]{1,0:T(8,128)(2,1)}, bf16[64,2048]{1,0:T(8,128)(2,1)S(1)}, u32[]{:S(2)}, u32[]{:S(2)}) collective-permute-start(bf16[64,2048]{1,0:T(8,128)(2,1)} %get-tuple-element.32), channel_id=1, source_target_pairs={{0,1},{1,2},{2,3},{3,0},{4,5},{5,6},{6,7},{7,4},{8,9},{9,10},{10,1... | collective-permute-start | bytes 786440 | tf_op jit(solution)/shard_map/ppermute | solution.py:285
  (22 other events, 207.5 us)
